TPU v7x, 256 devices: a whole 4x4x8 slice. The times are simulated.
256 devices in a mesh: seq: 64 (over x, y_lo, z), ch: 4 (over y_hi, core).
Axes of the slice: x: 4, y: 4 (y_hi: 2, y_lo: 2; y = y_hi * 2 + y_lo), z: 8, core: 2. Of those that a mesh axis runs over, the one named last changes fastest.
Arguments:
- projected: bfloat16 [8192, 3, 4096], P('seq', None, 'ch'), may hold values from -6 to 6
- cotangent: bfloat16 [8192, 4096], P('seq', 'ch'), may hold values from -6 to 6
- short_weight: float32 [3, 7, 4096], P(None, None, 'ch'), may hold values from -2 to 2
- long_filter: float32 [8, 8192], P('ch', 'seq'), may hold values from -0.0625 to 0.0625
Outputs:
- grad_proj: bfloat16 [8192, 3, 4096], P('seq', None, 'ch')
- grad_short: float32 [3, 7, 4096], P(None, None, 'ch')
- grad_filter: float32 [8, 8192], P(None, ('seq', 'ch'))
All inputs are finite; a program needn't handle non-finite values.
Results may differ from a plain program's by a relative error of at most 0.00155.
Values may be sent and summed in bfloat16 or wider, within the bound.
No kernel may reach another device: no remote copies, remote signals or barrier semaphores. Data moves between devices by JAX's collectives and lax.ppermute only.
A program may use at most 64 MiB of HBM per device.

v0:
```python
import math

import jax
import jax.numpy as jnp
from jax import lax
from jax.sharding import PartitionSpec as P

highest = lax.Precision.HIGHEST


def passed_along(block, axis, distance):
    devices = range(lax.axis_size(axis))
    route = [(i - distance, i) for i in devices if i - distance in devices]
    return lax.ppermute(block, axis, route)


def einsum_high(form, table, operand):
    return jnp.einsum(form, table, operand, precision=highest)


def angle_table(first, second, length):
    product = first[:, None] * second[None, :] % length
    radians = product.astype(jnp.float32) * (2.0 * math.pi / length)
    return (jnp.cos(radians), jnp.sin(radians))


def complex_dft(cosine, sine, real_part, imag_part, joined, sign):
    table = jnp.stack(
        [jnp.stack([cosine, -sign * sine], 0), jnp.stack([sign * sine, cosine], 0)], 0
    )
    stacked = jnp.stack([real_part, imag_part], 0)
    result = jnp.einsum(joined, table, stacked, precision=highest)
    return (result[0], result[1])


def rotate(real_part, imag_part, cosine, sine, sign):
    return (
        real_part * cosine - sign * imag_part * sine,
        imag_part * cosine + sign * real_part * sine,
    )


def combine(mixed_re, mixed_im, grad_re, grad_im, filt_re, filt_im):
    conv_re = filt_re * mixed_re - filt_im * mixed_im
    conv_im = filt_re * mixed_im + filt_im * mixed_re
    corr_re = filt_re * grad_re + filt_im * grad_im
    corr_im = filt_re * grad_im - filt_im * grad_re
    cross_re = mixed_re * grad_re + mixed_im * grad_im
    cross_im = mixed_re * grad_im - mixed_im * grad_re
    return (conv_re - corr_im, conv_im + corr_re, cross_re, cross_im)


def featurize(extended, weights, row_count):
    tap_count = weights.shape[1]
    accumulated = jnp.zeros((row_count,) + extended.shape[1:], jnp.float32)
    for offset in range(tap_count):
        first_row = tap_count - 1 - offset
        accumulated = accumulated + weights[:, offset, :] * extended[
            first_row : first_row + row_count
        ].astype(jnp.float32)
    return accumulated


def transpose_pair(signals, filters):
    return (
        lax.all_to_all(signals, "seq", split_axis=0, concat_axis=1, tiled=True),
        lax.all_to_all(filters, "seq", split_axis=0, concat_axis=1, tiled=True),
    )


def sequence_plan(mixed_input, gated_grad, long_filter):
    row_count, chan_count = mixed_input.shape
    group_count = long_filter.shape[0]
    seq_count = lax.axis_size("seq")
    seq_index = lax.axis_index("seq")
    per_block = row_count // seq_count
    fft_length = 2 * row_count * seq_count
    freq_index = jnp.arange(2 * seq_count, dtype=jnp.int32)
    block_index = jnp.arange(seq_count, dtype=jnp.int32)
    row_index = jnp.arange(row_count, dtype=jnp.int32)
    signals = jnp.stack([mixed_input, gated_grad], 1)[:, None]
    filters = jnp.transpose(long_filter)[:, None]
    sig_cols, filt_cols = transpose_pair(signals, filters)
    cos_one, sin_one = angle_table(freq_index, block_index, 2 * seq_count)
    sig_re = einsum_high("kb,abxc->kaxc", cos_one, sig_cols)
    sig_im = -einsum_high("kb,abxc->kaxc", sin_one, sig_cols)
    filt_re = einsum_high("kb,abg->kag", cos_one, filt_cols)
    filt_im = -einsum_high("kb,abg->kag", sin_one, filt_cols)
    positions = seq_index * per_block + jnp.arange(per_block, dtype=jnp.int32)
    cos_twist, sin_twist = angle_table(freq_index, positions, fft_length)
    sig_re, sig_im = rotate(
        sig_re, sig_im, cos_twist[:, :, None, None], sin_twist[:, :, None, None], -1.0
    )
    filt_re, filt_im = rotate(filt_re, filt_im, cos_twist[:, :, None], sin_twist[:, :, None], -1.0)
    sig_rows, filt_rows = transpose_pair(
        jnp.stack([sig_re, sig_im], 2), jnp.stack([filt_re, filt_im], 2)
    )
    cos_two, sin_two = angle_table(row_index, row_index, row_count)
    spec_re, spec_im = complex_dft(
        cos_two, sin_two, sig_rows[:, :, 0], sig_rows[:, :, 1], "pqka,qjaxc->pjkxc", -1.0
    )
    hspec_re, hspec_im = complex_dft(
        cos_two, sin_two, filt_rows[:, :, 0], filt_rows[:, :, 1], "pqka,qjag->pjkg", -1.0
    )
    leading = spec_re.shape[:2]
    group_shape = leading + (group_count, chan_count // group_count)
    wave_re, wave_im, cross_re, cross_im = combine(
        spec_re[:, :, 0].reshape(group_shape),
        spec_im[:, :, 0].reshape(group_shape),
        spec_re[:, :, 1].reshape(group_shape),
        spec_im[:, :, 1].reshape(group_shape),
        hspec_re[..., None],
        hspec_im[..., None],
    )
    wave_re = wave_re.reshape(leading + (chan_count,))
    wave_im = wave_im.reshape(leading + (chan_count,))
    cross_re = jnp.sum(cross_re, -1)
    cross_im = jnp.sum(cross_im, -1)
    back_re, back_im = complex_dft(cos_two, sin_two, wave_re, wave_im, "pqak,qjkc->pajc", 1.0)
    cback_re, cback_im = complex_dft(cos_two, sin_two, cross_re, cross_im, "pqak,qjkg->pajg", 1.0)
    pair_freq = seq_index * 2 + jnp.arange(2, dtype=jnp.int32)
    cos_back, sin_back = angle_table(row_index, pair_freq, fft_length)
    back_re, back_im = rotate(back_re, back_im, cos_back[:, :, None], sin_back[:, :, None], 1.0)
    cback_re, cback_im = rotate(cback_re, cback_im, cos_back[:, :, None], sin_back[:, :, None], 1.0)
    wave_cols, cross_cols = transpose_pair(
        jnp.stack([back_re, back_im], 2), jnp.stack([cback_re, cback_im], 2)
    )
    cos_three, sin_three = angle_table(block_index, freq_index, 2 * seq_count)
    time_re, time_im = complex_dft(
        cos_three, sin_three, wave_cols[:, :, 0], wave_cols[:, :, 1], "pqbk,qakc->pbac", 1.0
    )
    cross_time = einsum_high("bk,akg->bag", cos_three, cross_cols[:, :, 0]) - einsum_high(
        "bk,akg->bag", sin_three, cross_cols[:, :, 1]
    )
    inverse_scale = 1.0 / fft_length
    wave_out, cross_out = transpose_pair(
        jnp.stack([time_re, time_im], 2) * inverse_scale, cross_time * inverse_scale
    )
    return (wave_out[0, :, 0], wave_out[0, :, 1], jnp.transpose(cross_out[0]))


def local(projected, cotangent, short_weight, long_filter):
    tap_count = short_weight.shape[1]
    row_count = projected.shape[0]
    margin = tap_count - 1
    front_rows = passed_along(projected[row_count - margin :], "seq", 1)
    extended = jnp.concatenate([front_rows, projected], 0)
    features = featurize(extended, short_weight, row_count)
    grad_out = cotangent.astype(jnp.float32)
    mixed_input = features[:, 1] * features[:, 2]
    gated_grad = grad_out * features[:, 0]
    conv_out, corr_out, filt_grad = sequence_plan(mixed_input, gated_grad, long_filter)
    token_count = row_count * lax.axis_size("seq")
    group_width = mixed_input.shape[1] // long_filter.shape[0]
    scaled_grad = filt_grad * (1.0 / math.sqrt(token_count * group_width))
    owned_grad = lax.all_to_all(scaled_grad, "ch", split_axis=1, concat_axis=0, tiled=True)
    feat_grad = jnp.stack(
        [grad_out * conv_out, corr_out * features[:, 2], corr_out * features[:, 1]], 1
    )
    next_rows = passed_along(feat_grad[:margin].astype(jnp.bfloat16), "seq", -1).astype(jnp.float32)
    extended_grad = jnp.concatenate([feat_grad, next_rows], 0)
    grad_proj = jnp.zeros(feat_grad.shape, jnp.float32)
    for offset in range(tap_count):
        grad_proj = (
            grad_proj + short_weight[:, offset, :] * extended_grad[offset : offset + row_count]
        )
    short_terms = []
    for offset in range(tap_count):
        first_row = margin - offset
        short_terms.append(
            jnp.sum(feat_grad * extended[first_row : first_row + row_count].astype(jnp.float32), 0)
        )
    grad_short = lax.psum(jnp.stack(short_terms, 1), "seq") * (1.0 / math.sqrt(token_count))
    return (grad_proj.astype(jnp.bfloat16), grad_short, owned_grad)


def solution(mesh):
    return jax.shard_map(
        local,
        mesh=mesh,
        in_specs=(P("seq", None, "ch"), P("seq", "ch"), P(None, None, "ch"), P("ch", "seq")),
        out_specs=(P("seq", None, "ch"), P(None, None, "ch"), P(None, ("seq", "ch"))),
        check_vma=False,
    )
```

profile of v0, /device:TPU:16, one launch (start us, length us, event | category | flops | bytes accessed | tf_op | source)
XLA Modules:
  0.0 929.5 jit_solution(14938506437671617002)
XLA Ops:
  8.1 3.8 collective-permute-start
  13.4 11.8 %all-to-all-start = ((f32[128,1,2]{2,1,0:T(1,128)}), f32[128,1,2]{2,1,0:T(1,128)S(1)}, u32[]{:S(2)}, u32[]{:S(2)}) async-start(f32[128,1,2]{2,1,0:T(1,128)} %bitcast.9), calls=%async_computation | async-start | bytes 131072 | tf_op jit(solution)/shard_map/all_to_all | solution.py:67
  28.6 5.6 fusion.9
  38.0 11.2 %all-to-all-start.2 = ((f32[128,1,2,1024]{3,2,1,0:T(2,128)}), f32[128,1,2,1024]{3,2,1,0:T(2,128)S(1)}, u32[]{:S(2)}, u32[]{:S(2)}) async-start(f32[128,1,2,1024]{3,2,1,0:T(2,128)} %copy.147), calls=%async_computation.2 | async-start | bytes 2097152 | tf_op jit(solution)/shard_map/all_to_all | solution.py:66
  51.5 25.5 %all-to-all-done.2 = f32[128,1,2,1024]{3,2,1,0:T(2,128)S(1)} async-done(((f32[128,1,2,1024]{3,2,1,0:T(2,128)}), f32[128,1,2,1024]{3,2,1,0:T(2,128)S(1)}, u32[]{:S(2)}, u32[]{:S(2)}) %all-to-all-start.2) | async-done | bytes 1048608 | tf_op jit(solution)/shard_map/all_to_all | solution.py:66
  77.1 6.5 all-to-all-start.1
  86.0 2.9 subtract_bitcast_fusion
  89.4 5.2 copy.149
  95.8 10.6 %all-to-all-start.3 = ((f32[128,2,2,2,1024]{4,3,1,2,0:T(2,128)}), f32[128,2,2,2,1024]{4,3,1,2,0:T(2,128)}, u32[]{:S(2)}, u32[]{:S(2)}) async-start(f32[128,2,2,2,1024]{4,3,1,2,0:T(2,128)} %copy.149), calls=%async_computation.3 | async-start | bytes 8388608 | tf_op jit(solution)/shard_map/all_to_all | solution.py:66
  110.6 88.6 %all-to-all-done.3 = f32[128,2,2,2,1024]{4,3,1,2,0:T(2,128)} async-done(((f32[128,2,2,2,1024]{4,3,1,2,0:T(2,128)}), f32[128,2,2,2,1024]{4,3,1,2,0:T(2,128)}, u32[]{:S(2)}, u32[]{:S(2)}) %all-to-all-start.3) | async-done | bytes 4194336 | tf_op jit(solution)/shard_map/all_to_all | solution.py:66
  199.2 4.2 copy.150
  203.4 3.6 fusion.141
  207.0 2.8 copy.212
  209.8 4.1 copy.213
  213.9 5.1 fusion.3
  229.8 8.1 all-to-all-start.6
  242.2 7.7 all-to-all-done.6
  249.9 2.7 copy.199
  255.5 4.6 all-to-all-start.7
  260.4 3.0 copy.156
  263.3 7.4 all-to-all-done.7
  270.8 4.7 all-to-all-start.4
  276.8 44.4 %all-to-all-done.4 = f32[128,2,2,1024]{3,1,2,0:T(2,128)S(1)} async-done(((f32[128,2,2,1024]{3,1,2,0:T(2,128)}), f32[128,2,2,1024]{3,1,2,0:T(2,128)S(1)}, u32[]{:S(2)}, u32[]{:S(2)}) %all-to-all-start.4) | async-done | bytes 2097184 | tf_op jit(solution)/shard_map/all_to_all | solution.py:66
  321.2 5.0 all-to-all-start.8
  328.3 2.7 all_to_all.127
  334.5 6.7 all-to-all-start.5
  341.2 29.2 %all-to-all-done.5 = f32[64,2,2,1024]{3,1,2,0:T(2,128)S(1)} async-done(((f32[64,2,2,1024]{3,1,2,0:T(2,128)}), f32[64,2,2,1024]{3,1,2,0:T(2,128)S(1)}, u32[]{:S(2)}, u32[]{:S(2)}) %all-to-all-start.5) | async-done | bytes 1048608 | tf_op jit(solution)/shard_map/all_to_all | solution.py:66
  371.8 2.6 fusion.140
  375.9 5.4 fusion.16
  385.1 3.7 collective-permute-done.1
  390.2 3.8 fusion.18
  395.2 525.0 %all-reduce.2.cloned.1.call-done = f32[3,7,1024]{2,0,1:T(4,128)} async-done(((f32[3,7,1024]{2,0,1:T(4,128)}), f32[3,7,1024]{2,0,1:T(4,128)}) %all-reduce.2.cloned.1.call-update) | async-done | bytes 86032 | tf_op jit(solution)/shard_map/psum | solution.py:173
  (131 shorter events, 56.6 us)
Async XLA Ops:
  7.2 21.5 %copy-start.2 = (bf16[128,3,1024]{2,0,1:T(8,128)(2,1)S(1)}, bf16[128,3,1024]{2,0,1:T(8,128)(2,1)}, u32[]{:S(2)}) copy-start(bf16[128,3,1024]{2,0,1:T(8,128)(2,1)} %param.4) | copy-start | bytes 2359300
  8.1 18.6 %collective-permute-start = (bf16[6,3,1024]{2,1,0:T(4,128)(2,1)S(1)}, bf16[6,3,1024]{2,1,0:T(4,128)(2,1)S(1)}, u32[]{:S(2)}, u32[]{:S(2)}) collective-permute-start(bf16[6,3,1024]{2,1,0:T(4,128)(2,1)S(1)} %copy.248), channel_id=1, source_target_pairs={{0,4},{4,8},{8,12},{12,16},{16,20},{20,24},{24,28},{28,32},{32,36}... | collective-permute-start | bytes 110600 | tf_op jit(solution)/shard_map/ppermute | solution.py:14
  13.4 24.6 %all-to-all-start = ((f32[128,1,2]{2,1,0:T(1,128)}), f32[128,1,2]{2,1,0:T(1,128)S(1)}, u32[]{:S(2)}, u32[]{:S(2)}) async-start(f32[128,1,2]{2,1,0:T(1,128)} %bitcast.9), calls=%async_computation | async-start | bytes 131072 | tf_op jit(solution)/shard_map/all_to_all | solution.py:67
  26.7 7.6 copy-start.11
  34.3 1.4 copy-start.1
  34.3 1.4 copy-start.8
  35.4 0.8 copy-start.4
  38.0 39.1 %all-to-all-start.2 = ((f32[128,1,2,1024]{3,2,1,0:T(2,128)}), f32[128,1,2,1024]{3,2,1,0:T(2,128)S(1)}, u32[]{:S(2)}, u32[]{:S(2)}) async-start(f32[128,1,2,1024]{3,2,1,0:T(2,128)} %copy.147), calls=%async_computation.2 | async-start | bytes 2097152 | tf_op jit(solution)/shard_map/all_to_all | solution.py:66
  50.0 36.0 %copy-start.13 = (f32[128,2]{0,1:T(2,128)}, f32[128,2]{0,1:T(2,128)S(1)}, u32[]{:S(2)}) copy-start(f32[128,2]{0,1:T(2,128)S(1)} %get-tuple-element.73) | copy-start | bytes 3076
  77.1 18.8 %all-to-all-start.1 = ((f32[128,2,2,2]{3,1,2,0:T(2,128)}), f32[128,2,2,2]{3,1,2,0:T(2,128)S(1)}, u32[]{:S(2)}, u32[]{:S(2)}) async-start(f32[128,2,2,2]{3,1,2,0:T(2,128)} %copy.137), calls=%async_computation.1 | async-start | bytes 524288 | tf_op jit(solution)/shard_map/all_to_all | solution.py:67
  95.8 103.3 %all-to-all-start.3 = ((f32[128,2,2,2,1024]{4,3,1,2,0:T(2,128)}), f32[128,2,2,2,1024]{4,3,1,2,0:T(2,128)}, u32[]{:S(2)}, u32[]{:S(2)}) async-start(f32[128,2,2,2,1024]{4,3,1,2,0:T(2,128)} %copy.149), calls=%async_computation.3 | async-start | bytes 8388608 | tf_op jit(solution)/shard_map/all_to_all | solution.py:66
  219.2 1.4 copy-start
  222.2 3.8 copy-start.6
  222.2 3.8 copy-start.7
  229.8 20.1 %all-to-all-start.6 = ((f32[128,2,2,2]{3,1,2,0:T(2,128)}), f32[128,2,2,2]{3,1,2,0:T(2,128)}, u32[]{:S(2)}, u32[]{:S(2)}) async-start(f32[128,2,2,2]{3,1,2,0:T(2,128)} %copy.168), calls=%async_computation.6 | async-start | bytes 524288 | tf_op jit(solution)/shard_map/all_to_all | solution.py:67
  239.9 2.0 copy-start.14
  239.9 2.0 copy-start.15
  255.5 15.3 %all-to-all-start.7 = ((f32[64,2,2]{2,1,0:T(2,128)}), f32[64,2,2]{2,1,0:T(2,128)S(1)}, u32[]{:S(2)}, u32[]{:S(2)}) async-start(f32[64,2,2]{2,1,0:T(2,128)} %copy.173), calls=%async_computation.7 | async-start | bytes 131072 | tf_op jit(solution)/shard_map/all_to_all | solution.py:67
  270.8 50.4 %all-to-all-start.4 = ((f32[128,2,2,1024]{3,1,2,0:T(2,128)}), f32[128,2,2,1024]{3,1,2,0:T(2,128)S(1)}, u32[]{:S(2)}, u32[]{:S(2)}) async-start(f32[128,2,2,1024]{3,1,2,0:T(2,128)} %copy.156), calls=%async_computation.4 | async-start | bytes 4194304 | tf_op jit(solution)/shard_map/all_to_all | solution.py:66
  321.2 13.3 %all-to-all-start.8 = ((f32[2,4,32]{2,0,1:T(2,128)}), f32[2,4,32]{2,0,1:T(2,128)S(1)}, u32[]{:S(2)}, u32[]{:S(2)}) async-start(f32[2,4,32]{2,0,1:T(2,128)} %copy.176), calls=%async_computation.8 | async-start | bytes 8192 | tf_op jit(solution)/shard_map/all_to_all | solution.py:156
  334.5 35.9 %all-to-all-start.5 = ((f32[64,2,2,1024]{3,1,2,0:T(2,128)}), f32[64,2,2,1024]{3,1,2,0:T(2,128)S(1)}, u32[]{:S(2)}, u32[]{:S(2)}) async-start(f32[64,2,2,1024]{3,1,2,0:T(2,128)} %copy.159), calls=%async_computation.5 | async-start | bytes 2097152 | tf_op jit(solution)/shard_map/all_to_all | solution.py:66
  341.1 579.1 %all-reduce.2.cloned.1.call-start = ((), (), s32[]{:S(2)}) async-start(), calls=%async_computation.9 | async-start | bytes 229376 | tf_op jit(solution)/shard_map/psum | solution.py:173
  370.9 3.5 copy-start.5
  371.8 3.4 copy-start.9
  374.6 1.3 copy-start.3
  382.8 6.0 collective-permute-start.1
  384.3 5.9 copy-start.12
  384.4 0.6 copy-start.10
Sparse Core Ops, SparseCore 0:
  385.2 534.9 all-reduce.1
where the time goes:
time: 937 us; the launch traced here: 929 us
  waiting for transfers between devices  733 us (78%)
  starting transfers between devices  74.5 us (8%)
  local copies, waits for them, and re-layouts  57.2 us (6%)
  other arithmetic  34.2 us (4%)
  matrix products  16 us (2%)
  between operations  15 us (2%)
    psum x1, waiting for transfers between devices, local(): lax.psum(jnp.stack(short_terms, 1), 'seq') * (1.0 / math.sqrt(token_count))  525 us
    all_to_all x4, waiting for transfers between devices, transpose_pair(): lax.all_to_all(signals, 'seq', split_axis=0, concat_axis=1, tiled=True)  188 us
    all_to_all x4, starting transfers between devices, transpose_pair(): lax.all_to_all(signals, 'seq', split_axis=0, concat_axis=1, tiled=True)  33.2 us
    all_to_all x4, starting transfers between devices, transpose_pair(): lax.all_to_all(filters, 'seq', split_axis=0, concat_axis=1, tiled=True)  30.9 us
  transfers between devices with their start and end apart: 12, of which 9 were waited for; matrix products, arithmetic and copies ran while one was open for 6% of the time, Pallas kernels for 0%

commit v1 on v0

v1 whole, which is shorter than its diff:
```python
import math

import jax
import jax.numpy as jnp
from jax import lax
from jax.experimental import pallas as pl
from jax.experimental.pallas import tpu as pltpu
from jax.sharding import PartitionSpec as P

f32 = jnp.float32
bf16 = jnp.bfloat16

BLK = 128
NBLK = 64
CH = 16
TAPS = 7
ROWS_IN = 72
ROWS_OUT = 56


def iota(shape, dim):
    return lax.broadcasted_iota(jnp.int32, shape, dim)


def split(x):
    hi = x.astype(bf16)
    return hi, (x - hi.astype(f32)).astype(bf16)


def flip_matrix(n):
    return jnp.where(iota((n, n), 0) + iota((n, n), 1) == n - 1, 1.0, 0.0).astype(bf16)


def dot(a, b):
    return jnp.dot(a, b, preferred_element_type=f32)


def pack_kernel(proj, cot, filt, out):
    for stream in range(4):
        block = proj[stream] if stream < 3 else cot[...]
        turned = block.astype(f32).T.astype(bf16)
        out[:, stream * CH : (stream + 1) * CH, :] = turned.reshape(NBLK, CH, BLK)
    row = iota((8, BLK), 0)
    for group in range(2):
        taps = filt[group : group + 1, :]
        hi = taps.astype(bf16).astype(f32)
        lo = taps - hi
        tile = jnp.where(row == 0, hi, jnp.where(row == 1, lo, 0.0)).astype(bf16)
        half = NBLK // 2
        out[group * half : (group + 1) * half, 4 * CH : ROWS_IN, :] = jnp.broadcast_to(
            tile[None], (half, 8, BLK)
        )


def main_kernel(
    recv, wide, out, toep_hi, toep_lo, zed, mixed, mixt, gsp, gleft, feat1, feat2, acc, crs, corr, diag, rrev, rlow, grads
):
    lane = iota((CH, BLK), 1)
    lane_sq = iota((BLK, BLK), 1)
    row_sq = iota((BLK, BLK), 0)
    keep = lane_sq >= row_sq
    flip2 = flip_matrix(2 * BLK)
    flip1 = flip_matrix(BLK)

    toep_hi[0] = jnp.zeros((BLK, BLK), bf16)
    toep_lo[0] = jnp.zeros((BLK, BLK), bf16)

    def build(m, before):
        pair = recv[m, 4 * CH : ROWS_IN, :].astype(f32)
        taps = pair[0:1] + pair[1:2]
        turned = pltpu.roll(jnp.broadcast_to(taps, (BLK, BLK)), 0, 1, stride=1, stride_axis=0)
        hi, lo = split(jnp.where(keep, turned, before))
        toep_hi[m + 1] = hi
        toep_lo[m + 1] = lo
        return turned

    lax.fori_loop(0, NBLK, build, jnp.zeros((BLK, BLK), f32))

    def featurize(pair_index, before):
        for half in range(2):
            b = pair_index * 2 + half
            current = tuple(recv[b, j * CH : (j + 1) * CH, :].astype(f32) for j in range(3))
            feats = []
            for j in range(3):
                total = wide[j * TAPS] * current[j]
                for k in range(1, TAPS):
                    source = jnp.where(lane < BLK - k, current[j], before[j])
                    total = total + wide[j * TAPS + k] * pltpu.roll(source, k, 1)
                feats.append(total)
            feat1[b] = feats[1]
            feat2[b] = feats[2]
            mix = feats[1] * feats[2]
            gate = recv[b, 3 * CH : 4 * CH, :].astype(f32) * feats[0]
            cols = slice(half * BLK, (half + 1) * BLK)
            cols_lo = slice((2 + half) * BLK, (3 + half) * BLK)
            at = pl.ds(pl.multiple_of(pair_index * CH, CH), CH)
            mixed[at, cols] = mix
            hi, lo = split(mix)
            at_z = pl.ds(pl.multiple_of(pair_index * 2 * CH, CH), CH)
            zed[at_z, cols] = hi
            zed[at_z, cols_lo] = lo
            hi, lo = split(gate)
            gsp[at, cols] = hi
            gsp[at, cols_lo] = lo
            before = current
        return before

    zero = jnp.zeros((CH, BLK), f32)
    lax.fori_loop(0, NBLK // 2, featurize, (zero, zero, zero))

    rows = NBLK // 2 * CH
    width = 2 * BLK
    for part in range(rows // BLK):
        at = slice(part * BLK, (part + 1) * BLK)
        hi, lo = split(mixed[at, :].T)
        mixt[0, :, at] = hi
        mixt[1, :, at] = lo
    for half in range(2):
        cols = slice(half * width, (half + 1) * width)
        gleft[half, 0:rows, :] = dot(gsp[:, cols], flip2).astype(bf16)
        gleft[half, rows : 2 * rows, :] = jnp.zeros((rows, width), bf16)
        for b in range(NBLK // 2):
            back = NBLK // 2 - 1 - b
            zed[2 * CH * back + CH : 2 * CH * back + 2 * CH, cols] = gleft[half, b * CH : (b + 1) * CH, :]

    last = None
    for d in range(NBLK // 2):
        depth = rows if d < NBLK // 4 else rows // 2
        at = slice(CH * d, CH * d + depth)
        left = jnp.concatenate([mixt[0, :, 0:depth], mixt[1, :, 0:depth], mixt[0, :, 0:depth]], 1)
        right = jnp.concatenate([gleft[0, at, :], gleft[0, at, :], gleft[1, at, :]], 0)
        prod = dot(left, right)
        diag[2 * d] = prod[0:BLK, BLK:] + prod[BLK:, 0:BLK]
        if d > 0:
            diag[2 * d - 1] = last + prod[BLK:, BLK:]
        last = prod[0:BLK, 0:BLK]
    diag[NBLK - 1] = last

    def along(step, after):
        q = NBLK - 1 - step
        turned = pltpu.roll(diag[q], 0, 1, stride=1, stride_axis=0)
        picked = jnp.where(keep, turned, after)
        rrev[pl.ds(q, 1), :] = jnp.sum(picked, 0, keepdims=True)
        return turned

    lax.fori_loop(0, NBLK, along, jnp.zeros((BLK, BLK), f32))
    hi, lo = split(rrev[...])
    rrev[0:NBLK, :] = dot(hi, flip1)
    rlow[...] = dot(lo, flip1)

    for d in range(NBLK // 2):
        count = 2 * rows - 2 * CH * d
        hi = jnp.concatenate(
            [
                jnp.concatenate([toep_hi[2 * d + 1], toep_hi[2 * d + 2]], 1),
                jnp.concatenate([toep_hi[2 * d], toep_hi[2 * d + 1]], 1),
            ],
            0,
        )
        lo = jnp.concatenate(
            [
                jnp.concatenate([toep_lo[2 * d + 1], toep_lo[2 * d + 2]], 1),
                jnp.concatenate([toep_lo[2 * d], toep_lo[2 * d + 1]], 1),
            ],
            0,
        )
        left = jnp.concatenate([zed[0:count, :], zed[0:count, 0:width]], 1)
        prod = dot(left, jnp.concatenate([hi, hi, lo], 0))
        if d == 0:
            acc[...] = prod
        else:
            acc[2 * CH * d :, :] = acc[2 * CH * d :, :] + prod
    for b in range(NBLK // 2):
        back = NBLK // 2 - 1 - b
        hi, lo = split(acc[2 * CH * back + CH : 2 * CH * back + 2 * CH, :])
        crs[b * CH : (b + 1) * CH, 0:width] = hi
        crs[b * CH : (b + 1) * CH, width:] = lo
    corr[...] = dot(crs[:, 0:width], flip2) + dot(crs[:, width:], flip2)

    def feat_grad(pair_index, carry):
        for half in range(2):
            b = pair_index * 2 + half
            cols = slice(half * BLK, (half + 1) * BLK)
            conv_part = acc[pl.ds(pl.multiple_of(pair_index * 2 * CH, CH), CH), cols]
            corr_part = corr[pl.ds(pl.multiple_of(pair_index * CH, CH), CH), cols]
            grads[0, b] = recv[b, 3 * CH : 4 * CH, :].astype(f32) * conv_part
            grads[1, b] = corr_part * feat2[b]
            grads[2, b] = corr_part * feat1[b]
        return carry

    lax.fori_loop(0, NBLK // 2, feat_grad, 0)
    short = jnp.zeros((CH, BLK), f32)
    for j in range(3):
        grads[j, NBLK] = zero

        def finish(b, sums, j=j):
            here, there = grads[j, b], grads[j, b + 1]
            given = recv[b, j * CH : (j + 1) * CH, :].astype(f32)
            total = wide[j * TAPS] * here
            fresh = [sums[0] + here * given]
            for k in range(1, TAPS):
                moved = pltpu.roll(jnp.where(lane >= k, here, there), BLK - k, 1)
                total = total + wide[j * TAPS + k] * moved
                fresh.append(sums[k] + moved * given)
            out[b, j * CH : (j + 1) * CH, :] = total.astype(bf16)
            return tuple(fresh)

        sums = lax.fori_loop(0, NBLK, finish, (zero,) * TAPS)
        for k in range(TAPS):
            short = jnp.where(lane == j * TAPS + k, jnp.sum(sums[k], 1, keepdims=True), short)

    row8 = iota((8, BLK), 0)
    tile = jnp.zeros((8, BLK), f32)
    mine = lane % CH == iota((CH, BLK), 0)
    for place, piece in enumerate(split(short)):
        for r in range(3):
            pick = jnp.where(row_sq == 8 * r + lane_sq // CH, 1.0, 0.0).astype(bf16)
            flat = jnp.sum(jnp.where(mine, dot(piece, pick), 0.0), 0, keepdims=True)
            tile = jnp.where(row8 == 2 + 3 * place + r, flat, tile)

    def tail(d, carry):
        high = rrev[pl.ds(d, 1), :]
        low = rlow[pl.ds(d, 1), :]
        whole = jnp.where(row8 == 0, high, jnp.where(row8 == 1, low, tile))
        out[d, 3 * CH : ROWS_OUT, :] = whole.astype(bf16)
        return carry

    lax.fori_loop(0, NBLK, tail, 0)


def unpack_kernel(recv, proj, short, filt):
    for j in range(3):
        block = recv[:, j * CH : (j + 1) * CH, :].reshape(NBLK * CH, BLK)
        proj[j] = block.astype(f32).T.astype(bf16)
    tail = recv[:, 3 * CH : ROWS_OUT, :].astype(f32)
    short[...] = tail[:, 2:5, :] + tail[:, 5:8, :]
    half = NBLK // 2
    for group in range(2):
        part = tail[group * half : (group + 1) * half]
        total = jnp.sum(part, 0)
        filt[group : group + 1, :] = total[0:1] + total[1:2]


def call(kernel, out_shape, scratch=()):
    return pl.pallas_call(kernel, out_shape=out_shape, scratch_shapes=list(scratch))


def pack(proj, cot, filt):
    return call(pack_kernel, jax.ShapeDtypeStruct((NBLK, ROWS_IN, BLK), bf16))(proj, cot, filt)


def middle(recv, wide, interpret=False):
    rows = NBLK // 2 * CH
    width = 2 * BLK
    vmem = pltpu.VMEM
    return pl.pallas_call(
        main_kernel,
        out_shape=jax.ShapeDtypeStruct((NBLK, ROWS_OUT, BLK), bf16),
        scratch_shapes=[
            vmem((NBLK + 1, BLK, BLK), bf16),
            vmem((NBLK + 1, BLK, BLK), bf16),
            vmem((2 * rows, 2 * width), bf16),
            vmem((rows, width), f32),
            vmem((2, width, rows), bf16),
            vmem((rows, 2 * width), bf16),
            vmem((2, 2 * rows, width), bf16),
            vmem((NBLK, CH, BLK), f32),
            vmem((NBLK, CH, BLK), f32),
            vmem((2 * rows, width), f32),
            vmem((rows, 2 * width), bf16),
            vmem((rows, width), f32),
            vmem((NBLK, BLK, BLK), f32),
            vmem((NBLK, BLK), f32),
            vmem((NBLK, BLK), f32),
            vmem((3, NBLK + 1, CH, BLK), f32),
        ],
        interpret=interpret,
    )(recv, wide)


def local(projected, cotangent, short_weight, long_filter):
    chan_count = projected.shape[2]
    token_count = BLK * NBLK
    sent = pack(jnp.transpose(projected, (1, 0, 2)), cotangent, long_filter)
    recv = lax.all_to_all(sent, "seq", split_axis=0, concat_axis=0, tiled=True)
    mine = lax.dynamic_slice_in_dim(
        short_weight.reshape(3 * TAPS, chan_count), lax.axis_index("seq") * CH, CH, 1
    )
    wide = jnp.broadcast_to(mine[:, :, None], (3 * TAPS, CH, BLK))
    back = middle(recv, wide)
    back = lax.all_to_all(back, "seq", split_axis=0, concat_axis=0, tiled=True)
    proj, short, filt = call(
        unpack_kernel,
        (
            jax.ShapeDtypeStruct((3, BLK, chan_count), bf16),
            jax.ShapeDtypeStruct((NBLK, 3, BLK), f32),
            jax.ShapeDtypeStruct((2, BLK), f32),
        ),
    )(back)
    grad_proj = jnp.transpose(proj, (1, 0, 2))
    short = jnp.transpose(short.reshape(NBLK, 24, CH), (1, 0, 2)).reshape(24, chan_count)
    grad_short = short[: 3 * TAPS].reshape(3, TAPS, chan_count) * (1.0 / math.sqrt(token_count))
    filt = filt * (1.0 / math.sqrt(token_count * (chan_count // 2)))
    grad_filter = lax.all_to_all(filt, "ch", split_axis=1, concat_axis=0, tiled=True)
    return (grad_proj, grad_short, grad_filter)


def solution(mesh):
    return jax.shard_map(
        local,
        mesh=mesh,
        in_specs=(P("seq", None, "ch"), P("seq", "ch"), P(None, None, "ch"), P("ch", "seq")),
        out_specs=(P("seq", None, "ch"), P(None, None, "ch"), P(None, ("seq", "ch"))),
        check_vma=False,
    )
```

time: 937 us -> 146 us (0.16)
  the two profiles are of different devices: /device:TPU:16 before, /device:TPU:1 now
where the time goes in v1:
time: 146 us; the launch traced here: 145 us
  Pallas kernels  53.7 us (37%)
  waiting for transfers between devices  32.1 us (22%)
  blocking collectives  30.7 us (21%)
  starting transfers between devices  22.6 us (15%)
  local copies, waits for them, and re-layouts  4.74 us (3%)
    pallas_call x1, Pallas kernels, middle(): pl.pallas_call(main_kernel, out_shape=jax.ShapeDtypeStruct((NBLK, ROWS_OU...  48.8 us
    all_to_all x1, blocking collectives, local(): back = lax.all_to_all(back, 'seq', split_axis=0, concat_axis=0, tiled=True)  30.7 us
    all_to_all x1, waiting for transfers between devices, local(): recv = lax.all_to_all(sent, 'seq', split_axis=0, concat_axis=0, tiled=True)  28.8 us
    all_to_all x1, starting transfers between devices, local(): recv = lax.all_to_all(sent, 'seq', split_axis=0, concat_axis=0, tiled=True)  13.6 us
    all_to_all x1, starting transfers between devices, local(): lax.all_to_all(filt, 'ch', split_axis=1, concat_axis=0, tiled=True)  9.01 us
    all_to_all x1, waiting for transfers between devices, local(): lax.all_to_all(filt, 'ch', split_axis=1, concat_axis=0, tiled=True)  3.31 us
  transfers between devices with their start and end apart: 2, of which 2 were waited for; matrix products, arithmetic and copies ran while one was open for 1% of the time, Pallas kernels for 0%

profile of v1, /device:TPU:1, one launch (start us, length us, event | category | flops | bytes accessed | tf_op | source)
XLA Modules:
  0.0 145.3 jit_solution(8948830729392192493)
XLA Ops:
  0.6 2.6 %shard_map.67 = bf16[64,72,128]{2,1,0:T(8,128)(2,1)} custom-call(bf16[3,128,1024]{2,1,0:T(8,128)(2,1)} %bitcast.8, bf16[128,1024]{1,0:T(8,128)(2,1)} %cot.1, f32[2,128]{1,0:T(2,128)} %filt.1), custom_call_target="tpu_custom_call" | custom-call | tf_op jit(solution)/shard_map/pallas_call | solution.py:249
  3.2 0.0 copy-start.1
  3.2 13.6 %all-to-all-start = ((bf16[64,72,128]{2,1,0:T(8,128)(2,1)}), bf16[64,72,128]{2,1,0:T(8,128)(2,1)S(1)}, u32[]{:S(2)}, u32[]{:S(2)}) async-start(bf16[64,72,128]{2,1,0:T(8,128)(2,1)} %shard_map.67), calls=%async_computation | async-start | bytes 2359296 | tf_op jit(solution)/shard_map/all_to_all | solution.py:285
  16.9 0.0 copy-done.1
  16.9 0.1 constant_dynamic-slice_fusion
  17.0 28.8 %all-to-all-done.recv = bf16[64,72,128]{2,1,0:T(8,128)(2,1)S(1)} async-done(((bf16[64,72,128]{2,1,0:T(8,128)(2,1)}), bf16[64,72,128]{2,1,0:T(8,128)(2,1)S(1)}, u32[]{:S(2)}, u32[]{:S(2)}) %all-to-all-start) | async-done | bytes 1179680 | tf_op jit(solution)/shard_map/all_to_all | solution.py:285
  45.8 0.0 copy-start
  45.8 0.9 broadcast_in_dim.2.wide
  46.7 0.2 copy-done
  46.8 48.8 %shard_map.68 = bf16[64,56,128]{2,1,0:T(8,128)(2,1)} custom-call(bf16[64,72,128]{2,1,0:T(8,128)(2,1)} %copy-done, f32[21,16,128]{2,1,0:T(8,128)} %broadcast_in_dim.2.wide), custom_call_target="tpu_custom_call" | custom-call | tf_op jit(solution)/shard_map/pallas_call | solution.py:256
  95.6 30.7 %all_to_all.29.recv = bf16[64,56,128]{2,1,0:T(8,128)(2,1)} all-to-all(bf16[64,56,128]{2,1,0:T(8,128)(2,1)} %shard_map.68), channel_id=1, replica_groups=mesh['seq'=64,'ch'=4] {'seq'}, dimensions={0} | all-to-all | bytes 1835008 | tf_op jit(solution)/shard_map/all_to_all | solution.py:291
  126.3 2.4 %shard_map.69 = (bf16[3,128,1024]{2,1,0:T(8,128)(2,1)}, f32[64,3,128]{2,1,0:T(4,128)}, f32[2,128]{1,0:T(2,128)}) custom-call(bf16[64,56,128]{2,1,0:T(8,128)(2,1)} %all_to_all.29.recv), custom_call_target="tpu_custom_call" | custom-call | tf_op jit(solution)/shard_map/pallas_call | solution.py:292
  128.7 1.0 copy.12
  129.7 0.7 broadcast_multiply_fusion
  130.4 0.1 all_to_all.22
  130.5 0.6 copy.14
  131.1 9.0 %all-to-all-start.2 = ((f32[2,4,32]{2,0,1:T(2,128)}), f32[2,4,32]{2,0,1:T(2,128)S(1)}, u32[]{:S(2)}, u32[]{:S(2)}) async-start(f32[2,4,32]{2,0,1:T(2,128)} %copy.14), calls=%async_computation.2 | async-start | bytes 8192 | tf_op jit(solution)/shard_map/all_to_all | solution.py:304
  140.1 0.3 copy.13
  140.4 1.0 mul.21
  141.4 3.3 %all-to-all-done.2 = f32[2,4,32]{2,0,1:T(2,128)S(1)} async-done(((f32[2,4,32]{2,0,1:T(2,128)}), f32[2,4,32]{2,0,1:T(2,128)S(1)}, u32[]{:S(2)}, u32[]{:S(2)}) %all-to-all-start.2) | async-done | bytes 1056 | tf_op jit(solution)/shard_map/all_to_all | solution.py:304
  144.7 0.6 copy.16
  (2 shorter events, 0.0 us)
Async XLA Ops:
  3.2 13.6 %copy-start.1 = (f32[3,7,1024]{2,1,0:T(8,128)S(1)}, f32[3,7,1024]{2,1,0:T(8,128)}, u32[]{:S(2)}) copy-start(f32[3,7,1024]{2,1,0:T(8,128)} %param.6) | copy-start | bytes 258052
  3.2 42.5 %all-to-all-start = ((bf16[64,72,128]{2,1,0:T(8,128)(2,1)}), bf16[64,72,128]{2,1,0:T(8,128)(2,1)S(1)}, u32[]{:S(2)}, u32[]{:S(2)}) async-start(bf16[64,72,128]{2,1,0:T(8,128)(2,1)} %shard_map.67), calls=%async_computation | async-start | bytes 2359296 | tf_op jit(solution)/shard_map/all_to_all | solution.py:285
  45.8 1.1 copy-start
  131.1 13.6 %all-to-all-start.2 = ((f32[2,4,32]{2,0,1:T(2,128)}), f32[2,4,32]{2,0,1:T(2,128)S(1)}, u32[]{:S(2)}, u32[]{:S(2)}) async-start(f32[2,4,32]{2,0,1:T(2,128)} %copy.14), calls=%async_computation.2 | async-start | bytes 8192 | tf_op jit(solution)/shard_map/all_to_all | solution.py:304

commit v2 on v1

--- a/solution.py
+++ b/solution.py
@@ -74,7 +74,7 @@
         toep_lo[m + 1] = lo
         return turned
 
-    lax.fori_loop(0, NBLK, build, jnp.zeros((BLK, BLK), f32))
+    lax.fori_loop(0, NBLK, build, jnp.zeros((BLK, BLK), f32), unroll=8)
 
     def featurize(pair_index, before):
         for half in range(2):
@@ -106,7 +106,7 @@
         return before
 
     zero = jnp.zeros((CH, BLK), f32)
-    lax.fori_loop(0, NBLK // 2, featurize, (zero, zero, zero))
+    lax.fori_loop(0, NBLK // 2, featurize, (zero, zero, zero), unroll=4)
 
     rows = NBLK // 2 * CH
     width = 2 * BLK
@@ -143,7 +143,7 @@
         rrev[pl.ds(q, 1), :] = jnp.sum(picked, 0, keepdims=True)
         return turned
 
-    lax.fori_loop(0, NBLK, along, jnp.zeros((BLK, BLK), f32))
+    lax.fori_loop(0, NBLK, along, jnp.zeros((BLK, BLK), f32), unroll=8)
     hi, lo = split(rrev[...])
     rrev[0:NBLK, :] = dot(hi, flip1)
     rlow[...] = dot(lo, flip1)
@@ -188,7 +188,7 @@
             grads[2, b] = corr_part * feat1[b]
         return carry
 
-    lax.fori_loop(0, NBLK // 2, feat_grad, 0)
+    lax.fori_loop(0, NBLK // 2, feat_grad, 0, unroll=4)
     short = jnp.zeros((CH, BLK), f32)
     for j in range(3):
         grads[j, NBLK] = zero
@@ -205,7 +205,7 @@
             out[b, j * CH : (j + 1) * CH, :] = total.astype(bf16)
             return tuple(fresh)
 
-        sums = lax.fori_loop(0, NBLK, finish, (zero,) * TAPS)
+        sums = lax.fori_loop(0, NBLK, finish, (zero,) * TAPS, unroll=16)
         for k in range(TAPS):
             short = jnp.where(lane == j * TAPS + k, jnp.sum(sums[k], 1, keepdims=True), short)
 
@@ -225,24 +225,45 @@
         out[d, 3 * CH : ROWS_OUT, :] = whole.astype(bf16)
         return carry
 
-    lax.fori_loop(0, NBLK, tail, 0)
-
-
-def unpack_kernel(recv, proj, short, filt):
+    lax.fori_loop(0, NBLK, tail, 0, unroll=8)
+
+
+def reduce_kernel(tail, filt):
+    half = NBLK // 2
+    scale = 1.0 / math.sqrt(BLK * NBLK * CH * half)
+    row = iota((8, BLK), 0)
+    totals = []
+    for group in range(2):
+        total = jnp.sum(tail[group * half : (group + 1) * half].astype(f32), 0)
+        totals.append((total[0:1] + total[1:2]) * scale)
+    both = jnp.where(row == 0, totals[0], totals[1])
+    for piece in range(4):
+        filt[piece] = both if piece == 0 else pltpu.roll(both, BLK - piece * (BLK // 4), 1)
+
+
+def unpack_kernel(recv, proj, short):
+    chans = NBLK * CH
     for j in range(3):
-        block = recv[:, j * CH : (j + 1) * CH, :].reshape(NBLK * CH, BLK)
+        block = recv[:, j * CH : (j + 1) * CH, :].reshape(chans, BLK)
         proj[j] = block.astype(f32).T.astype(bf16)
     tail = recv[:, 3 * CH : ROWS_OUT, :].astype(f32)
-    short[...] = tail[:, 2:5, :] + tail[:, 5:8, :]
-    half = NBLK // 2
-    for group in range(2):
-        part = tail[group * half : (group + 1) * half]
-        total = jnp.sum(part, 0)
-        filt[group : group + 1, :] = total[0:1] + total[1:2]
-
-
-def call(kernel, out_shape, scratch=()):
-    return pl.pallas_call(kernel, out_shape=out_shape, scratch_shapes=list(scratch))
+    spread = jnp.where(iota((NBLK, chans), 1) // CH == iota((NBLK, chans), 0), 1.0, 0.0).astype(bf16)
+    own = iota((BLK, chans), 0) % CH == iota((BLK, chans), 1) % CH
+    gather = jnp.where(iota((8, BLK), 1) // CH == iota((8, BLK), 0), 1.0, 0.0).astype(bf16)
+    parts = []
+    for r in range(3):
+        total = jnp.zeros((8, chans), f32)
+        for place in range(2):
+            piece = tail[:, 2 + 3 * place + r, :].T.astype(bf16)
+            total = total + dot(gather, jnp.where(own, dot(piece, spread), 0.0).astype(bf16))
+        parts.append(total)
+    whole = jnp.concatenate(parts, 0) * (1.0 / math.sqrt(BLK * NBLK))
+    for j in range(3):
+        short[j] = whole[j * TAPS : (j + 1) * TAPS]
+
+
+def call(kernel, out_shape, **rest):
+    return pl.pallas_call(kernel, out_shape=out_shape, **rest)
 
 
 def pack(proj, cot, filt):
@@ -280,7 +301,6 @@
 
 def local(projected, cotangent, short_weight, long_filter):
     chan_count = projected.shape[2]
-    token_count = BLK * NBLK
     sent = pack(jnp.transpose(projected, (1, 0, 2)), cotangent, long_filter)
     recv = lax.all_to_all(sent, "seq", split_axis=0, concat_axis=0, tiled=True)
     mine = lax.dynamic_slice_in_dim(
@@ -289,19 +309,23 @@
     wide = jnp.broadcast_to(mine[:, :, None], (3 * TAPS, CH, BLK))
     back = middle(recv, wide)
     back = lax.all_to_all(back, "seq", split_axis=0, concat_axis=0, tiled=True)
-    proj, short, filt = call(
+    shares = call(
+        reduce_kernel,
+        jax.ShapeDtypeStruct((4, 8, BLK), f32),
+        grid=(1,),
+        in_specs=[pl.BlockSpec((NBLK, 8, BLK), lambda i: (0, 3 * CH // 8, 0))],
+        out_specs=pl.BlockSpec((4, 8, BLK), lambda i: (0, 0, 0)),
+    )(back)
+    owned = lax.all_to_all(shares, "ch", split_axis=0, concat_axis=0, tiled=True)
+    proj, grad_short = call(
         unpack_kernel,
         (
             jax.ShapeDtypeStruct((3, BLK, chan_count), bf16),
-            jax.ShapeDtypeStruct((NBLK, 3, BLK), f32),
-            jax.ShapeDtypeStruct((2, BLK), f32),
+            jax.ShapeDtypeStruct((3, TAPS, chan_count), f32),
         ),
     )(back)
     grad_proj = jnp.transpose(proj, (1, 0, 2))
-    short = jnp.transpose(short.reshape(NBLK, 24, CH), (1, 0, 2)).reshape(24, chan_count)
-    grad_short = short[: 3 * TAPS].reshape(3, TAPS, chan_count) * (1.0 / math.sqrt(token_count))
-    filt = filt * (1.0 / math.sqrt(token_count * (chan_count // 2)))
-    grad_filter = lax.all_to_all(filt, "ch", split_axis=1, concat_axis=0, tiled=True)
+    grad_filter = owned[:, 0:2, 0 : BLK // 4].reshape(8, BLK // 4)
     return (grad_proj, grad_short, grad_filter)
 
 

time: 146 us -> 118 us (0.81)
  Pallas kernels: 53.7 us -> 32 us
  local copies, waits for them, and re-layouts: 4.74 us -> 1.77 us
  waiting for transfers between devices: 32.1 us -> 30.2 us
    pallas_call x1, Pallas kernels: 48.8 us -> 24.6 us  [middle(): pl.pallas_call(main_kernel, out_shape=jax.ShapeDtypeStruct((NBLK, ROWS_OU...]
    all_to_all x1, waiting for transfers between devices: 3.31 us -> 1.44 us  [local(): lax.all_to_all(shares, 'ch', split_axis=0, concat_axis=0, tiled=True)]
    pallas_call x0 -> x1, Pallas kernels: none -> 1.61 us  [local(): call(reduce_kernel, jax.ShapeDtypeStruct((4, 8, BLK), f32), grid=(1,), in...]
  transfers between devices with their start and end apart: 2 -> 2, of which waited for: 2 -> 2; matrix products, arithmetic and copies ran while one was open for 1% -> 0% of each run, Pallas kernels for 0% -> 3%
where the time goes in v2:
time: 118 us
  Pallas kernels  32 us (27%)
  blocking collectives  30.7 us (26%)
  waiting for transfers between devices  30.2 us (26%)
  starting transfers between devices  22.6 us (19%)
  local copies, waits for them, and re-layouts  1.77 us (2%)
    all_to_all x1, blocking collectives, local(): back = lax.all_to_all(back, 'seq', split_axis=0, concat_axis=0, tiled=True)  30.7 us
    all_to_all x1, waiting for transfers between devices, local(): recv = lax.all_to_all(sent, 'seq', split_axis=0, concat_axis=0, tiled=True)  28.8 us
    pallas_call x1, Pallas kernels, middle(): pl.pallas_call(main_kernel, out_shape=jax.ShapeDtypeStruct((NBLK, ROWS_OU...  24.6 us
    all_to_all x1, starting transfers between devices, local(): recv = lax.all_to_all(sent, 'seq', split_axis=0, concat_axis=0, tiled=True)  13.6 us
    all_to_all x1, starting transfers between devices, local(): lax.all_to_all(shares, 'ch', split_axis=0, concat_axis=0, tiled=True)  9 us
    pallas_call x1, Pallas kernels, local(): call(unpack_kernel, (jax.ShapeDtypeStruct((3, BLK, chan_count), bf16), ja...  3.19 us
    pallas_call x1, Pallas kernels, pack(): call(pack_kernel, jax.ShapeDtypeStruct((NBLK, ROWS_IN, BLK), bf16))  2.59 us
  transfers between devices with their start and end apart: 2, of which 2 were waited for; matrix products, arithmetic and copies ran while one was open for 0% of the time, Pallas kernels for 3%

profile of v2, /device:TPU:1, one launch (start us, length us, event | category | flops | bytes accessed | tf_op | source)
XLA Modules:
  0.0 118.0 jit_solution(1468668394016157474)
XLA Ops:
  0.6 2.6 %shard_map.67 = bf16[64,72,128]{2,1,0:T(8,128)(2,1)} custom-call(bf16[3,128,1024]{2,1,0:T(8,128)(2,1)} %bitcast.3, bf16[128,1024]{1,0:T(8,128)(2,1)} %cot.1, f32[2,128]{1,0:T(2,128)} %filt.1), custom_call_target="tpu_custom_call" | custom-call | tf_op jit(solution)/shard_map/pallas_call | solution.py:270
  3.2 0.0 copy-start.1
  3.2 13.6 %all-to-all-start = ((bf16[64,72,128]{2,1,0:T(8,128)(2,1)}), bf16[64,72,128]{2,1,0:T(8,128)(2,1)S(1)}, u32[]{:S(2)}, u32[]{:S(2)}) async-start(bf16[64,72,128]{2,1,0:T(8,128)(2,1)} %shard_map.67), calls=%async_computation | async-start | bytes 2359296 | tf_op jit(solution)/shard_map/all_to_all | solution.py:305
  16.9 0.0 copy-done.1
  16.9 0.1 constant_dynamic-slice_fusion
  17.0 28.8 %all-to-all-done.recv = bf16[64,72,128]{2,1,0:T(8,128)(2,1)S(1)} async-done(((bf16[64,72,128]{2,1,0:T(8,128)(2,1)}), bf16[64,72,128]{2,1,0:T(8,128)(2,1)S(1)}, u32[]{:S(2)}, u32[]{:S(2)}) %all-to-all-start) | async-done | bytes 1179680 | tf_op jit(solution)/shard_map/all_to_all | solution.py:305
  45.8 0.0 copy-start
  45.8 0.9 broadcast_in_dim.2.wide
  46.7 0.2 copy-done
  46.8 24.6 %shard_map.68 = bf16[64,56,128]{2,1,0:T(8,128)(2,1)} custom-call(bf16[64,72,128]{2,1,0:T(8,128)(2,1)} %copy-done, f32[21,16,128]{2,1,0:T(8,128)} %broadcast_in_dim.2.wide), custom_call_target="tpu_custom_call" | custom-call | tf_op jit(solution)/shard_map/pallas_call | solution.py:277
  71.5 30.7 %all_to_all.15.recv.tail = bf16[64,56,128]{2,1,0:T(8,128)(2,1)} all-to-all(bf16[64,56,128]{2,1,0:T(8,128)(2,1)} %shard_map.68), channel_id=1, replica_groups=mesh['seq'=64,'ch'=4] {'seq'}, dimensions={0} | all-to-all | bytes 1835008 | tf_op jit(solution)/shard_map/all_to_all | solution.py:311
  102.2 1.6 %shard_map.70 = f32[4,8,128]{2,1,0:T(8,128)} custom-call(bf16[64,56,128]{2,1,0:T(8,128)(2,1)} %all_to_all.15.recv.tail), custom_call_target="tpu_custom_call" | custom-call | tf_op jit(solution)/shard_map/pallas_call | solution.py:312
  103.8 9.0 %all-to-all-start.2 = ((f32[4,8,128]{2,1,0:T(8,128)}), f32[4,8,128]{2,1,0:T(8,128)S(1)}, u32[]{:S(2)}, u32[]{:S(2)}) async-start(f32[4,8,128]{2,1,0:T(8,128)} %shard_map.70), calls=%async_computation.2 | async-start | bytes 32768 | tf_op jit(solution)/shard_map/all_to_all | solution.py:319
  112.8 3.2 %shard_map.69 = (bf16[3,128,1024]{2,1,0:T(8,128)(2,1)}, f32[3,7,1024]{2,1,0:T(8,128)}) custom-call(bf16[64,56,128]{2,1,0:T(8,128)(2,1)} %all_to_all.15.recv.tail), custom_call_target="tpu_custom_call" | custom-call | tf_op jit(solution)/shard_map/pallas_call | solution.py:320
  116.0 1.4 %all-to-all-done.2 = f32[4,8,128]{2,1,0:T(8,128)S(1)} async-done(((f32[4,8,128]{2,1,0:T(8,128)}), f32[4,8,128]{2,1,0:T(8,128)S(1)}, u32[]{:S(2)}, u32[]{:S(2)}) %all-to-all-start.2) | async-done | bytes 16416 | tf_op jit(solution)/shard_map/all_to_all | solution.py:319
  117.4 0.6 slice.4
  (1 shorter events, 0.0 us)
Async XLA Ops:
  3.2 13.6 %copy-start.1 = (f32[3,7,1024]{2,1,0:T(8,128)S(1)}, f32[3,7,1024]{2,1,0:T(8,128)}, u32[]{:S(2)}) copy-start(f32[3,7,1024]{2,1,0:T(8,128)} %param.6) | copy-start | bytes 258052
  3.2 42.5 %all-to-all-start = ((bf16[64,72,128]{2,1,0:T(8,128)(2,1)}), bf16[64,72,128]{2,1,0:T(8,128)(2,1)S(1)}, u32[]{:S(2)}, u32[]{:S(2)}) async-start(bf16[64,72,128]{2,1,0:T(8,128)(2,1)} %shard_map.67), calls=%async_computation | async-start | bytes 2359296 | tf_op jit(solution)/shard_map/all_to_all | solution.py:305
  45.8 1.1 copy-start
  103.8 13.6 %all-to-all-start.2 = ((f32[4,8,128]{2,1,0:T(8,128)}), f32[4,8,128]{2,1,0:T(8,128)S(1)}, u32[]{:S(2)}, u32[]{:S(2)}) async-start(f32[4,8,128]{2,1,0:T(8,128)} %shard_map.70), calls=%async_computation.2 | async-start | bytes 32768 | tf_op jit(solution)/shard_map/all_to_all | solution.py:319
